TPU v7x, 32 devices: a whole 2x2x4 slice. The times are simulated.
32 devices in a mesh: ctx: 8 (over z, x), tp: 4 (over y, core).
Axes of the slice: x: 2, y: 2, z: 4, core: 2. Of those that a mesh axis runs over, the one named last changes fastest.
Arguments:
- q_nope: bfloat16 [8, 128, 128], P('ctx', 'tp'), may hold values from -6 to 6
- q_rope: bfloat16 [8, 128, 64], P('ctx', 'tp'), may hold values from -256 to 256
- w_uk: bfloat16 [128, 128, 512], P('tp'), may hold values from -0.5 to 0.5
- w_uv: bfloat16 [128, 512, 128], P('tp'), may hold values from -3 to 3
- w_out: bfloat16 [16384, 7168], P('tp', 'ctx'), may hold values from -0.046875 to 0.046875
- prefix_cache: bfloat16 [32768, 576], P('ctx'), may hold values from -6 to 6
- block_table: int32 [512], P('ctx'), may hold values from 0 to 511, each once
- prefix_len: int32 [8], replicated, may hold values from 8192 to 32768
- suffix_cache: bfloat16 [8, 256, 576], P('ctx'), may hold values from -12 to 12
- suffix_len: int32 [8], P('ctx'), may hold values from 2 to 256
Outputs:
- layer_out: bfloat16 [8, 7168], P('tp', 'ctx')
Inputs may be any that keep to these rules, and one draw needn't show every extreme that they name: A permutation: slots b * 64 to b * 64 + 63 of prefix_cache hold prefix positions block_table[b] * 64 onwards.
All inputs are finite; a program needn't handle non-finite values.
Results may differ from a plain program's by a relative error of at most 0.0078.
Values may be sent and summed in bfloat16 or wider, within the bound.
A program may use at most 64 MiB of HBM per device.

v0:
```python
import jax
import jax.numpy as jnp
from jax import lax
from jax.sharding import PartitionSpec as P

LAT = 512
ROPE = 64
NOPE = 128
BLOCK = 64
masked_value = -1e30


def partial_stats(scores, visible, values, pattern):
    row_peak = jnp.max(jnp.where(visible, scores, masked_value), axis=2)
    weights = jnp.where(visible, jnp.exp(scores - row_peak[:, :, None]), 0.0).astype(jnp.bfloat16)
    row_mass = jnp.sum(weights, axis=2, dtype=jnp.float32)
    row_weighted = jnp.einsum(pattern, weights, values, preferred_element_type=jnp.float32)
    return (row_peak, row_mass, row_weighted)


def value_project(latent, value_weight):
    return jnp.einsum("rhc,hcv->rhv", latent, value_weight, precision=lax.Precision.HIGHEST)


def on_device(
    q_nope,
    q_rope,
    w_uk,
    w_uv,
    w_out,
    prefix_cache,
    block_table,
    prefix_len,
    suffix_cache,
    suffix_len,
):
    softmax_scale = (NOPE + ROPE) ** (-0.5)
    q_latent = jnp.einsum("rhn,hnc->rhc", q_nope, w_uk, preferred_element_type=jnp.float32).astype(
        jnp.bfloat16
    )
    own_queries = jnp.concatenate([q_latent, q_rope], axis=2)
    all_queries = lax.all_gather(own_queries, "ctx", axis=0, tiled=True)
    ctx_count = lax.axis_size("ctx")
    own_count = own_queries.shape[0]
    value_weight = w_uv.astype(jnp.float32)
    positions = (
        block_table[:, None] * BLOCK + jnp.arange(BLOCK, dtype=jnp.int32)[None, :]
    ).reshape(-1)
    visible = (positions[None, :] < prefix_len[:, None])[:, None, :]
    scores = (
        jnp.einsum("rhc,tc->rht", all_queries, prefix_cache, preferred_element_type=jnp.float32)
        * softmax_scale
    )
    row_peak, row_mass, row_weighted = partial_stats(
        scores, visible, prefix_cache[:, :LAT], "rht,tc->rhc"
    )
    suffix_scores = (
        jnp.einsum("rhc,rtc->rht", own_queries, suffix_cache, preferred_element_type=jnp.float32)
        * softmax_scale
    )
    suffix_slots = jnp.arange(suffix_cache.shape[1], dtype=jnp.int32)
    suffix_visible = (suffix_slots[None, :] < suffix_len[:, None])[:, None, :]
    tail_peak, tail_mass, tail_weighted = partial_stats(
        suffix_scores, suffix_visible, suffix_cache[:, :, :LAT], "rht,rtc->rhc"
    )

    def by_owner(values):
        return values.reshape((ctx_count, own_count) + values.shape[1:])

    got_peak, got_mass, got_weighted = (
        lax.all_to_all(by_owner(row_peak), "ctx", split_axis=0, concat_axis=0, tiled=True),
        lax.all_to_all(by_owner(row_mass), "ctx", split_axis=0, concat_axis=0, tiled=True),
        lax.all_to_all(by_owner(row_weighted), "ctx", split_axis=0, concat_axis=0, tiled=True),
    )
    highest = jnp.maximum(jnp.max(got_peak, axis=0), tail_peak)
    factors = jnp.exp(got_peak - highest[None])
    tail_factor = jnp.exp(tail_peak - highest)
    total_mass = jnp.sum(factors * got_mass, axis=0) + tail_factor * tail_mass
    total_weighted = (
        jnp.sum(factors[..., None] * got_weighted, axis=0) + tail_factor[:, :, None] * tail_weighted
    )
    head_values = value_project(total_weighted / total_mass[:, :, None], value_weight).astype(
        jnp.bfloat16
    )
    flat_values = head_values.reshape(own_count, -1)
    every_value = lax.all_gather(flat_values, "ctx", axis=0, tiled=True)
    return lax.psum_scatter(
        jnp.dot(every_value, w_out, preferred_element_type=jnp.float32),
        "tp",
        scatter_dimension=0,
        tiled=True,
    ).astype(jnp.bfloat16)


def solution(mesh):
    placed = (
        P("ctx", "tp", None),
        P("ctx", "tp", None),
        P("tp", None, None),
        P("tp", None, None),
        P("tp", "ctx"),
        P("ctx", None),
        P("ctx"),
        P(),
        P("ctx", None, None),
        P("ctx"),
    )
    return jax.shard_map(
        on_device, mesh=mesh, in_specs=placed, out_specs=P("tp", "ctx"), check_vma=False
    )
```

profile of v0, /device:TPU:0, one launch (start us, length us, event | category | flops | bytes accessed | tf_op | source)
XLA Modules:
  0.0 129.5 jit_solution(10840114998855403633)
XLA Ops:
  0.0 0.0 copy-start
  0.0 0.7 broadcast_multiply_fusion
  0.7 0.1 iota_add_fusion
  0.8 0.1 add.38
  0.9 0.0 copy-done
  0.9 3.0 %fusion.20 = bf16[32,1,512]{2,1,0:T(2,128)(2,1)S(1)} fusion(bf16[32,128,512]{2,1,0:T(8,128)(2,1)} %param.12, bf16[32,128,1]{1,0,2:T(8,128)(2,1)S(1)} %bitcast.55), kind=kOutput, calls=%fused_computation.32 | convolution fusion | flops 4194304 | bytes 4235264 | tf_op jit(solution)/shard_map/rhn,hnc->rhc/dot_general | solution.py:38
  3.9 0.0 copy-done.3
  3.9 32.7 %all_gather.6 = bf16[8,32,576]{2,1,0:T(8,128)(2,1)S(1)} all-gather(bf16[1,32,576]{2,1,0:T(8,128)(2,1)S(1)} %pad_maximum_fusion), channel_id=1, replica_groups=mesh['ctx'=8,'tp'=4] {'ctx'}, dimensions={0}, use_global_device_ids=true | all-gather | bytes 331776 | tf_op jit(solution)/shard_map/all_gather | solution.py:42
  36.6 0.0 copy-done.4
  36.6 0.1 broadcast_compare_fusion
  36.7 0.0 copy-done.5
  36.7 2.7 %select_reduce_fusion = (f32[8,32]{1,0:T(8,128)}, f32[8,32,4096]{2,1,0:T(8,128)S(1)}) fusion(pred[8,4096]{1,0:T(8,128)(4,1)S(1)} %broadcast_compare_fusion, bf16[8,32,576]{2,1,0:T(8,128)(2,1)S(1)} %all_gather.6, bf16[4096,576]{0,1:T(8,128)(2,1)S(1)} %copy-done.5), kind=kOutput, calls=%fused_computation.7 | convolution fusion | flops 1211105024 | bytes 9241600 | tf_op jit(solution)/shard_map/rhc,tc->rht/dot_general | solution.py:51
  39.4 1.9 %copy-done.1 = f32[8,32,4096]{2,1,0:T(8,128)} copy-done((f32[8,32,4096]{2,1,0:T(8,128)}, f32[8,32,4096]{2,1,0:T(8,128)S(1)}, u32[]{:S(2)}) %copy-start.1) | copy-done | bytes 4194328
  41.3 1.7 %convert_reduce_fusion = f32[8,32]{1,0:T(8,128)S(1)} fusion(f32[8,32,4096]{2,1,0:T(8,128)S(1)} %get-tuple-element.10, f32[8,32]{1,0:T(8,128)} %get-tuple-element.9, pred[8,4096]{1,0:T(8,128)(4,1)S(1)} %broadcast_compare_fusion), kind=kLoop, calls=%fused_computation.4 | loop fusion | flops 5242624 | bytes 4229120 | tf_op jit(solution)/shard_map/reduce_sum | solution.py:16
  43.0 11.8 %all_to_all.15 = f32[8,1,32]{2,1,0:T(1,128)S(1)} all-to-all(f32[8,1,32]{2,1,0:T(1,128)S(1)} %bitcast.60), channel_id=1, replica_groups=mesh['ctx'=8,'tp'=4] {'ctx'}, dimensions={0} | all-to-all | bytes 2048 | tf_op jit(solution)/shard_map/all_to_all | solution.py:72
  54.9 3.2 %all-to-all-start = ((f32[8,1,32]{2,1,0:T(1,128)}), f32[8,1,32]{2,1,0:T(1,128)S(1)}, u32[]{:S(2)}, u32[]{:S(2)}) async-start(f32[8,1,32]{2,1,0:T(1,128)} %bitcast.5), calls=%async_computation | async-start | bytes 8192 | tf_op jit(solution)/shard_map/all_to_all | solution.py:71
  58.1 0.0 copy-start.6
  58.1 0.0 copy-start.2
  58.1 5.6 %fusion.4 = f32[8,1,32,512]{3,2,1,0:T(8,128)} fusion(bf16[4096,576]{0,1:T(8,128)(2,1)} %param.15, f32[8,32,4096]{2,1,0:T(8,128)} %copy-done.1, f32[8,32]{1,0:T(8,128)} %get-tuple-element.9, pred[8,4096]{1,0:T(8,128)(4,1)S(1)} %broadcast_compare_fusion), kind=kOutput, calls=%fused_computation.8 | convolution fusion | flops 1076887552 | bytes 8949760 | tf_op jit(solution)/shard_map/rht,tc->rhc/dot_general | solution.py:17
  63.7 0.8 all-to-all-done
  64.5 5.1 %all-to-all-start.1 = ((f32[8,1,32,512]{3,2,1,0:T(8,128)}), f32[8,1,32,512]{3,2,1,0:T(8,128)S(1)}, u32[]{:S(2)}, u32[]{:S(2)}) async-start(f32[8,1,32,512]{3,2,1,0:T(8,128)} %fusion.4), calls=%async_computation.1 | async-start | bytes 1048576 | tf_op jit(solution)/shard_map/all_to_all | solution.py:73
  70.3 0.7 dynamic-slice
  71.7 0.3 select_reduce_fusion.1
  72.0 0.2 convert_reduce_fusion.1
  72.2 7.8 %all-to-all-done.1 = f32[8,1,32,512]{3,2,1,0:T(8,128)S(1)} async-done(((f32[8,1,32,512]{3,2,1,0:T(8,128)}), f32[8,1,32,512]{3,2,1,0:T(8,128)S(1)}, u32[]{:S(2)}, u32[]{:S(2)}) %all-to-all-start.1) | async-done | bytes 524320 | tf_op jit(solution)/shard_map/all_to_all | solution.py:73
  80.0 0.1 multiply_reduce_fusion
  80.1 0.2 fusion.9
  80.3 3.5 %fusion.16 = f32[32,1,128]{2,1,0:T(1,128)S(1)} fusion(bf16[32,512,128]{2,1,0:T(8,128)(2,1)} %param.13, f32[32,512,1]{1,0,2:T(8,128)S(1)} %fusion.9), kind=kOutput, calls=%fused_computation.22 | convolution fusion | flops 25165824 | bytes 4276224 | tf_op jit(solution)/shard_map/rhc,hcv->rhv/dot_general | solution.py:22
  83.9 30.5 %all-gather = bf16[8,1,4096]{2,1,0:T(2,128)(2,1)S(1)} all-gather(bf16[1,1,4096]{2,1,0:T(2,128)(2,1)S(1)} %reshape.166), channel_id=1, replica_groups=mesh['ctx'=8,'tp'=4] {'ctx'}, dimensions={0}, use_global_device_ids=true | all-gather | bytes 73728 | tf_op jit(solution)/shard_map/all_gather | solution.py:86
  114.4 4.1 %fusion.13 = f32[8,896]{1,0:T(8,128)S(1)} fusion(bf16[4096,896]{1,0:T(8,128)(2,1)} %param.14, bf16[8,1,4096]{2,1,0:T(2,128)(2,1)S(1)} %all-gather), kind=kOutput, calls=%fused_computation.18 | convolution fusion | flops 58720256 | bytes 7434240 | tf_op jit(solution)/shard_map/dot_general | solution.py:88
  118.6 10.3 %all-reduce = bf16[8,896]{1,0:T(8,128)(2,1)S(1)} all-reduce(f32[8,896]{1,0:T(8,128)S(1)} %fusion.13), channel_id=2, replica_groups=mesh['ctx'=8,'tp'=4] {'tp'}, use_global_device_ids=true, to_apply=%region_7.8.clone | all-reduce | flops 7168 | bytes 43008
  128.9 0.6 dynamic-slice_convert_fusion
  (15 shorter events, 0.1 us)
Async XLA Ops:
  0.0 0.9 copy-start
  0.0 3.9 %copy-start.3 = (bf16[1,32,64]{2,1,0:T(8,128)(2,1)S(1)}, bf16[1,32,64]{2,1,0:T(8,128)(2,1)}, u32[]{:S(2)}) copy-start(bf16[1,32,64]{2,1,0:T(8,128)(2,1)} %param.11) | copy-start | bytes 12292
  0.0 36.6 %copy-start.4 = (s32[8]{0:T(128)S(1)}, s32[8]{0:T(128)}, u32[]{:S(2)}) copy-start(s32[8]{0:T(128)} %param.17) | copy-start | bytes 100
  0.9 35.8 %copy-start.5 = (bf16[4096,576]{0,1:T(8,128)(2,1)S(1)}, bf16[4096,576]{0,1:T(8,128)(2,1)}, u32[]{:S(2)}) copy-start(bf16[4096,576]{0,1:T(8,128)(2,1)} %param.15) | copy-start | bytes 14155780
  39.4 1.9 %copy-start.1 = (f32[8,32,4096]{2,1,0:T(8,128)}, f32[8,32,4096]{2,1,0:T(8,128)S(1)}, u32[]{:S(2)}) copy-start(f32[8,32,4096]{2,1,0:T(8,128)S(1)} %get-tuple-element.10) | copy-start | bytes 12582916
  54.9 9.7 %all-to-all-start = ((f32[8,1,32]{2,1,0:T(1,128)}), f32[8,1,32]{2,1,0:T(1,128)S(1)}, u32[]{:S(2)}, u32[]{:S(2)}) async-start(f32[8,1,32]{2,1,0:T(1,128)} %bitcast.5), calls=%async_computation | async-start | bytes 8192 | tf_op jit(solution)/shard_map/all_to_all | solution.py:71
  58.1 12.2 %copy-start.6 = (u32[32]{0:T(128)S(1)}, u32[32]{0:T(128)}, u32[]{:S(2)}) copy-start(u32[32]{0:T(128)} %constant.17) | copy-start | bytes 388
  58.1 13.6 %copy-start.2 = (bf16[1,256,576]{1,2,0:T(8,128)(2,1)S(1)}, bf16[1,256,576]{1,2,0:T(8,128)(2,1)}, u32[]{:S(2)}) copy-start(bf16[1,256,576]{1,2,0:T(8,128)(2,1)} %param.18) | copy-start | bytes 884740
  64.5 15.5 %all-to-all-start.1 = ((f32[8,1,32,512]{3,2,1,0:T(8,128)}), f32[8,1,32,512]{3,2,1,0:T(8,128)S(1)}, u32[]{:S(2)}, u32[]{:S(2)}) async-start(f32[8,1,32,512]{3,2,1,0:T(8,128)} %fusion.4), calls=%async_computation.1 | async-start | bytes 1048576 | tf_op jit(solution)/shard_map/all_to_all | solution.py:73
where the time goes:
time: 130 us; the launch traced here: 129 us
  blocking collectives  85.4 us (66%)
  matrix products  19.4 us (15%)
  waiting for transfers between devices  8.58 us (7%)
  starting transfers between devices  8.34 us (6%)
  local copies, waits for them, and re-layouts  3.31 us (3%)
  other arithmetic  3 us (2%)
  between operations  1.49 us (1%)
    all_gather x1, blocking collectives, on_device(): all_queries = lax.all_gather(own_queries, 'ctx', axis=0, tiled=True)  32.7 us
    all_gather x1, blocking collectives, on_device(): every_value = lax.all_gather(flat_values, 'ctx', axis=0, tiled=True)  30.5 us
    all_to_all x1, blocking collectives, on_device(): lax.all_to_all(by_owner(row_mass), 'ctx', split_axis=0, concat_axis=0, ti...  11.8 us
    unnamed x1, blocking collectives  10.3 us
    all_to_all x1, waiting for transfers between devices, on_device(): lax.all_to_all(by_owner(row_weighted), 'ctx', split_axis=0, concat_axis=0...  7.78 us
    dot_general x2, matrix products, partial_stats(): jnp.einsum(pattern, weights, values, preferred_element_type=jnp.float32)  5.81 us
    all_to_all x1, starting transfers between devices, on_device(): lax.all_to_all(by_owner(row_weighted), 'ctx', split_axis=0, concat_axis=0...  5.12 us
    dot_general x1, matrix products, on_device(): jnp.dot(every_value, w_out, preferred_element_type=jnp.float32)  4.14 us
  transfers between devices with their start and end apart: 2, of which 2 were waited for; matrix products, arithmetic and copies ran while one was open for 5% of the time, Pallas kernels for 0%

commit v1 on v0

--- a/solution.py
+++ b/solution.py
@@ -83,7 +83,12 @@
         jnp.bfloat16
     )
     flat_values = head_values.reshape(own_count, -1)
-    every_value = lax.all_gather(flat_values, "ctx", axis=0, tiled=True)
+    ring = [flat_values]
+    for hop in range(7):
+        ring.append(lax.ppermute(ring[-1], "ctx", [(dev, (dev + 1) % 8) for dev in range(8)]))
+    every_value = jnp.roll(
+        jnp.concatenate(ring[::-1], axis=0), (lax.axis_index("ctx") + 1) * ring[0].shape[0], axis=0
+    )
     return lax.psum_scatter(
         jnp.dot(every_value, w_out, preferred_element_type=jnp.float32),
         "tp",

time: 130 us -> 143 us (1.10)
  waiting for transfers between devices: 8.58 us -> 54.8 us
  blocking collectives: 85.4 us -> 43 us
  starting transfers between devices: 8.34 us -> 15.8 us
  other arithmetic: 3 us -> 5.07 us
  matrix products: 19.4 us -> 21.2 us
  local copies, waits for them, and re-layouts: 3.31 us -> 1.69 us
    ppermute x0 -> x7, waiting for transfers between devices: none -> 42.2 us  [on_device(): lax.ppermute(ring[-1], 'ctx', [(dev, (dev + 1) % 8) for dev in range(8)])]
    all_gather x1 -> x0, blocking collectives: 30.5 us -> none  [on_device(): every_value = lax.all_gather(flat_values, 'ctx', axis=0, tiled=True)]
    all_to_all x1 -> x0, blocking collectives: 11.8 us -> none  [on_device(): lax.all_to_all(by_owner(row_mass), 'ctx', split_axis=0, concat_axis=0, ti...]
    all_to_all x0 -> x1, starting transfers between devices: none -> 3.33 us  [on_device(): lax.all_to_all(by_owner(row_mass), 'ctx', split_axis=0, concat_axis=0, ti...]
    all_to_all x1, starting transfers between devices: 3.22 us -> 5.56 us  [on_device(): lax.all_to_all(by_owner(row_peak), 'ctx', split_axis=0, concat_axis=0, ti...]
    reduce_sum x2, other arithmetic: 1.93 us -> 4.01 us  [partial_stats(): row_mass = jnp.sum(weights, axis=2, dtype=jnp.float32)]
    unnamed x16 -> x14, local copies, waits for them, and re-layouts: 2.63 us -> 0.62 us
    all_to_all x1, waiting for transfers between devices: 0.79 us -> 2.68 us  [on_device(): lax.all_to_all(by_owner(row_peak), 'ctx', split_axis=0, concat_axis=0, ti...]
  transfers between devices with their start and end apart: 2 -> 10, of which waited for: 2 -> 10; matrix products, arithmetic and copies ran while one was open for 5% -> 7% of each run, Pallas kernels for 0% -> 0%
where the time goes in v1:
time: 143 us
  waiting for transfers between devices  54.8 us (38%)
  blocking collectives  43 us (30%)
  matrix products  21.2 us (15%)
  starting transfers between devices  15.8 us (11%)
  other arithmetic  5.07 us (4%)
  local copies, waits for them, and re-layouts  1.69 us (1%)
  between operations  1.44 us (1%)
    ppermute x7, waiting for transfers between devices, on_device(): lax.ppermute(ring[-1], 'ctx', [(dev, (dev + 1) % 8) for dev in range(8)])  42.2 us
    all_gather x1, blocking collectives, on_device(): all_queries = lax.all_gather(own_queries, 'ctx', axis=0, tiled=True)  32.7 us
    unnamed x1, blocking collectives  10.3 us
    all_to_all x1, waiting for transfers between devices, on_device(): lax.all_to_all(by_owner(row_weighted), 'ctx', split_axis=0, concat_axis=0...  9.06 us
    dot_general x2, matrix products, partial_stats(): jnp.einsum(pattern, weights, values, preferred_element_type=jnp.float32)  5.81 us
    all_to_all x1, starting transfers between devices, on_device(): lax.all_to_all(by_owner(row_peak), 'ctx', split_axis=0, concat_axis=0, ti...  5.56 us
    all_to_all x1, starting transfers between devices, on_device(): lax.all_to_all(by_owner(row_weighted), 'ctx', split_axis=0, concat_axis=0...  5.25 us
    dot_general x1, matrix products, on_device(): jnp.einsum('rhc,tc->rht', all_queries, prefix_cache, preferred_element_ty...  4.53 us
  transfers between devices with their start and end apart: 10, of which 10 were waited for; matrix products, arithmetic and copies ran while one was open for 7% of the time, Pallas kernels for 0%

profile of v1, /device:TPU:0, one launch (start us, length us, event | category | flops | bytes accessed | tf_op | source)
XLA Modules:
  0.0 143.0 jit_solution(10552600363920445594)
XLA Ops:
  0.0 0.7 broadcast_multiply_fusion
  0.8 0.1 add.51
  0.9 3.0 %fusion.19 = bf16[32,1,512]{2,1,0:T(2,128)(2,1)S(1)} fusion(bf16[32,128,512]{2,1,0:T(8,128)(2,1)} %param.12, bf16[32,128,1]{1,0,2:T(8,128)(2,1)S(1)} %bitcast.58), kind=kOutput, calls=%fused_computation.32 | convolution fusion | flops 4194304 | bytes 4235264 | tf_op jit(solution)/shard_map/rhn,hnc->rhc/dot_general | solution.py:38
  3.9 32.7 %all_gather.3 = bf16[8,32,576]{2,1,0:T(8,128)(2,1)S(1)} all-gather(bf16[1,32,576]{2,1,0:T(8,128)(2,1)S(1)} %pad_maximum_fusion), channel_id=1, replica_groups=mesh['ctx'=8,'tp'=4] {'ctx'}, dimensions={0}, use_global_device_ids=true | all-gather | bytes 331776 | tf_op jit(solution)/shard_map/all_gather | solution.py:42
  36.6 0.1 broadcast_compare_fusion
  36.7 4.5 %select_reduce_fusion = (f32[8,32]{1,0:T(8,128)}, f32[8,32,4096]{2,1,0:T(8,128)}) fusion(pred[8,4096]{1,0:T(8,128)(4,1)S(1)} %broadcast_compare_fusion, bf16[8,32,576]{2,1,0:T(8,128)(2,1)S(1)} %all_gather.3, bf16[4096,576]{0,1:T(8,128)(2,1)S(1)} %copy-done.4), kind=kOutput, calls=%fused_computation.7 | convolution fusion | flops 1211105024 | bytes 9241600 | tf_op jit(solution)/shard_map/rhc,tc->rht/dot_general | solution.py:51
  41.2 5.6 %all-to-all-start = ((f32[8,1,32]{2,1,0:T(1,128)}), f32[8,1,32]{2,1,0:T(1,128)S(1)}, u32[]{:S(2)}, u32[]{:S(2)}) async-start(f32[8,1,32]{2,1,0:T(1,128)} %bitcast.5), calls=%async_computation | async-start | bytes 8192 | tf_op jit(solution)/shard_map/all_to_all | solution.py:71
  46.8 3.8 %convert_reduce_fusion = f32[8,32]{1,0:T(8,128)} fusion(f32[8,32,4096]{2,1,0:T(8,128)} %get-tuple-element.10, f32[8,32]{1,0:T(8,128)} %get-tuple-element.9, pred[8,4096]{1,0:T(8,128)(4,1)S(1)} %broadcast_compare_fusion), kind=kLoop, calls=%fused_computation.4 | loop fusion | flops 5242624 | bytes 4229120 | tf_op jit(solution)/shard_map/reduce_sum | solution.py:16
  50.6 2.7 %all-to-all-done = f32[8,1,32]{2,1,0:T(1,128)S(1)} async-done(((f32[8,1,32]{2,1,0:T(1,128)}), f32[8,1,32]{2,1,0:T(1,128)S(1)}, u32[]{:S(2)}, u32[]{:S(2)}) %all-to-all-start) | async-done | bytes 1056 | tf_op jit(solution)/shard_map/all_to_all | solution.py:71
  53.2 3.3 %all-to-all-start.2 = ((f32[8,1,32]{2,1,0:T(1,128)}), f32[8,1,32]{2,1,0:T(1,128)S(1)}, u32[]{:S(2)}, u32[]{:S(2)}) async-start(f32[8,1,32]{2,1,0:T(1,128)} %bitcast.14), calls=%async_computation.2 | async-start | bytes 8192 | tf_op jit(solution)/shard_map/all_to_all | solution.py:72
  56.6 5.6 %fusion.4 = f32[8,1,32,512]{3,2,1,0:T(8,128)} fusion(bf16[4096,576]{0,1:T(8,128)(2,1)} %param.15, f32[8,32,4096]{2,1,0:T(8,128)} %get-tuple-element.10, f32[8,32]{1,0:T(8,128)} %get-tuple-element.9, pred[8,4096]{1,0:T(8,128)(4,1)S(1)} %broadcast_compare_fusion), kind=kOutput, calls=%fused_computation.8 | convolution fusion | flops 1076887552 | bytes 8949760 | tf_op jit(solution)/shard_map/rht,tc->rhc/dot_general | solution.py:17
  62.2 0.9 all-to-all-done.2
  63.1 5.3 %all-to-all-start.1 = ((f32[8,1,32,512]{3,2,1,0:T(8,128)}), f32[8,1,32,512]{3,2,1,0:T(8,128)S(1)}, u32[]{:S(2)}, u32[]{:S(2)}) async-start(f32[8,1,32,512]{3,2,1,0:T(8,128)} %fusion.4), calls=%async_computation.1 | async-start | bytes 1048576 | tf_op jit(solution)/shard_map/all_to_all | solution.py:73
  69.0 0.3 select_reduce_fusion.1
  69.3 0.2 convert_reduce_fusion.1
  69.5 9.1 %all-to-all-done.1 = f32[8,1,32,512]{3,2,1,0:T(8,128)S(1)} async-done(((f32[8,1,32,512]{3,2,1,0:T(8,128)}), f32[8,1,32,512]{3,2,1,0:T(8,128)S(1)}, u32[]{:S(2)}, u32[]{:S(2)}) %all-to-all-start.1) | async-done | bytes 524320 | tf_op jit(solution)/shard_map/all_to_all | solution.py:73
  78.6 0.1 multiply_reduce_fusion
  78.7 0.2 fusion.9
  78.9 3.5 %fusion.13 = f32[32,1,128]{2,1,0:T(1,128)S(1)} fusion(bf16[32,512,128]{2,1,0:T(8,128)(2,1)} %param.13, f32[32,512,1]{1,0,2:T(8,128)S(1)} %fusion.9), kind=kOutput, calls=%fused_computation.19 | convolution fusion | flops 25165824 | bytes 4276224 | tf_op jit(solution)/shard_map/rhc,hcv->rhv/dot_general | solution.py:22
  82.5 1.7 %collective-permute-start = (bf16[1,4096]{1,0:T(2,128)(2,1)S(1)}, bf16[1,4096]{1,0:T(2,128)(2,1)S(1)}, u32[]{:S(2)}, u32[]{:S(2)}) collective-permute-start(bf16[1,4096]{1,0:T(2,128)(2,1)S(1)} %bitcast.61), channel_id=1, source_target_pairs={{0,4},{4,8},{8,12},{12,16},{16,20},{20,24},{24,28},{28,0},{1,5},{5... | collective-permute-start | bytes 24584 | tf_op jit(solution)/shard_map/ppermute | solution.py:88
  84.2 4.8 %collective-permute-done = bf16[1,4096]{1,0:T(2,128)(2,1)S(1)} collective-permute-done((bf16[1,4096]{1,0:T(2,128)(2,1)S(1)}, bf16[1,4096]{1,0:T(2,128)(2,1)S(1)}, u32[]{:S(2)}, u32[]{:S(2)}) %collective-permute-start) | collective-permute-done | bytes 8224 | tf_op jit(solution)/shard_map/ppermute | solution.py:88
  88.9 6.4 %collective-permute-done.1 = bf16[1,4096]{1,0:T(2,128)(2,1)S(1)} collective-permute-done((bf16[1,4096]{1,0:T(2,128)(2,1)S(1)}, bf16[1,4096]{1,0:T(2,128)(2,1)S(1)}, u32[]{:S(2)}, u32[]{:S(2)}) %collective-permute-start.1) | collective-permute-done | bytes 8224 | tf_op jit(solution)/shard_map/ppermute | solution.py:88
  95.4 6.4 %collective-permute-done.2 = bf16[1,4096]{1,0:T(2,128)(2,1)S(1)} collective-permute-done((bf16[1,4096]{1,0:T(2,128)(2,1)S(1)}, bf16[1,4096]{1,0:T(2,128)(2,1)S(1)}, u32[]{:S(2)}, u32[]{:S(2)}) %collective-permute-start.2) | collective-permute-done | bytes 8224 | tf_op jit(solution)/shard_map/ppermute | solution.py:88
  101.8 6.4 %collective-permute-done.3 = bf16[1,4096]{1,0:T(2,128)(2,1)S(1)} collective-permute-done((bf16[1,4096]{1,0:T(2,128)(2,1)S(1)}, bf16[1,4096]{1,0:T(2,128)(2,1)S(1)}, u32[]{:S(2)}, u32[]{:S(2)}) %collective-permute-start.3) | collective-permute-done | bytes 8224 | tf_op jit(solution)/shard_map/ppermute | solution.py:88
  108.3 6.4 %collective-permute-done.4 = bf16[1,4096]{1,0:T(2,128)(2,1)S(1)} collective-permute-done((bf16[1,4096]{1,0:T(2,128)(2,1)S(1)}, bf16[1,4096]{1,0:T(2,128)(2,1)S(1)}, u32[]{:S(2)}, u32[]{:S(2)}) %collective-permute-start.4) | collective-permute-done | bytes 8224 | tf_op jit(solution)/shard_map/ppermute | solution.py:88
  114.7 6.4 %collective-permute-done.5 = bf16[1,4096]{1,0:T(2,128)(2,1)S(1)} collective-permute-done((bf16[1,4096]{1,0:T(2,128)(2,1)S(1)}, bf16[1,4096]{1,0:T(2,128)(2,1)S(1)}, u32[]{:S(2)}, u32[]{:S(2)}) %collective-permute-start.5) | collective-permute-done | bytes 8224 | tf_op jit(solution)/shard_map/ppermute | solution.py:88
  121.1 0.6 dynamic-slice
  122.4 5.2 %collective-permute-done.6 = bf16[1,4096]{1,0:T(2,128)(2,1)S(1)} collective-permute-done((bf16[1,4096]{1,0:T(2,128)(2,1)S(1)}, bf16[1,4096]{1,0:T(2,128)(2,1)S(1)}, u32[]{:S(2)}, u32[]{:S(2)}) %collective-permute-start.6) | collective-permute-done | bytes 8224 | tf_op jit(solution)/shard_map/ppermute | solution.py:88
  127.6 0.4 concatenate.10
  128.0 4.1 %fusion.15 = f32[8,896]{1,0:T(8,128)S(1)} fusion(bf16[4096,896]{1,0:T(8,128)(2,1)} %param.14, bf16[16,4096]{1,0:T(8,128)(2,1)S(1)} %concatenate.10, s32[]{:T(128)S(6)} %select_n.34), kind=kOutput, calls=%fused_computation.21 | convolution fusion | flops 58720256 | bytes 7434244 | tf_op jit(solution)/shard_map/dot_general | solution.py:93
  132.1 10.3 %all-reduce = bf16[8,896]{1,0:T(8,128)(2,1)S(1)} all-reduce(f32[8,896]{1,0:T(8,128)S(1)} %fusion.15), channel_id=2, replica_groups=mesh['ctx'=8,'tp'=4] {'tp'}, use_global_device_ids=true, to_apply=%region_7.8.clone | all-reduce | flops 7168 | bytes 43008
  142.4 0.6 dynamic-slice_convert_fusion
  (28 shorter events, 0.2 us)
Async XLA Ops:
  0.0 0.9 copy-start
  0.0 3.9 %copy-start.2 = (bf16[1,32,64]{2,1,0:T(8,128)(2,1)S(1)}, bf16[1,32,64]{2,1,0:T(8,128)(2,1)}, u32[]{:S(2)}) copy-start(bf16[1,32,64]{2,1,0:T(8,128)(2,1)} %param.11) | copy-start | bytes 12292
  0.0 36.6 %copy-start.3 = (s32[8]{0:T(128)S(1)}, s32[8]{0:T(128)}, u32[]{:S(2)}) copy-start(s32[8]{0:T(128)} %param.17) | copy-start | bytes 100
  0.9 35.8 %copy-start.4 = (bf16[4096,576]{0,1:T(8,128)(2,1)S(1)}, bf16[4096,576]{0,1:T(8,128)(2,1)}, u32[]{:S(2)}) copy-start(bf16[4096,576]{0,1:T(8,128)(2,1)} %param.15) | copy-start | bytes 14155780
  41.2 12.0 %all-to-all-start = ((f32[8,1,32]{2,1,0:T(1,128)}), f32[8,1,32]{2,1,0:T(1,128)S(1)}, u32[]{:S(2)}, u32[]{:S(2)}) async-start(f32[8,1,32]{2,1,0:T(1,128)} %bitcast.5), calls=%async_computation | async-start | bytes 8192 | tf_op jit(solution)/shard_map/all_to_all | solution.py:71
  53.2 9.8 %all-to-all-start.2 = ((f32[8,1,32]{2,1,0:T(1,128)}), f32[8,1,32]{2,1,0:T(1,128)S(1)}, u32[]{:S(2)}, u32[]{:S(2)}) async-start(f32[8,1,32]{2,1,0:T(1,128)} %bitcast.14), calls=%async_computation.2 | async-start | bytes 8192 | tf_op jit(solution)/shard_map/all_to_all | solution.py:72
  56.6 12.4 %copy-start.1 = (bf16[1,256,576]{1,2,0:T(8,128)(2,1)S(1)}, bf16[1,256,576]{1,2,0:T(8,128)(2,1)}, u32[]{:S(2)}) copy-start(bf16[1,256,576]{1,2,0:T(8,128)(2,1)} %param.18) | copy-start | bytes 884740
  62.2 58.9 %copy-start.5 = (u32[32]{0:T(128)S(1)}, u32[32]{0:T(128)}, u32[]{:S(2)}) copy-start(u32[32]{0:T(128)} %constant.47) | copy-start | bytes 388
  63.1 15.5 %all-to-all-start.1 = ((f32[8,1,32,512]{3,2,1,0:T(8,128)}), f32[8,1,32,512]{3,2,1,0:T(8,128)S(1)}, u32[]{:S(2)}, u32[]{:S(2)}) async-start(f32[8,1,32,512]{3,2,1,0:T(8,128)} %fusion.4), calls=%async_computation.1 | async-start | bytes 1048576 | tf_op jit(solution)/shard_map/all_to_all | solution.py:73
  82.5 6.5 %collective-permute-start = (bf16[1,4096]{1,0:T(2,128)(2,1)S(1)}, bf16[1,4096]{1,0:T(2,128)(2,1)S(1)}, u32[]{:S(2)}, u32[]{:S(2)}) collective-permute-start(bf16[1,4096]{1,0:T(2,128)(2,1)S(1)} %bitcast.61), channel_id=1, source_target_pairs={{0,4},{4,8},{8,12},{12,16},{16,20},{20,24},{24,28},{28,0},{1,5},{5... | collective-permute-start | bytes 24584 | tf_op jit(solution)/shard_map/ppermute | solution.py:88
  88.9 6.4 %collective-permute-start.1 = (bf16[1,4096]{1,0:T(2,128)(2,1)S(1)}, bf16[1,4096]{1,0:T(2,128)(2,1)S(1)}, u32[]{:S(2)}, u32[]{:S(2)}) collective-permute-start(bf16[1,4096]{1,0:T(2,128)(2,1)S(1)} %collective-permute-done), channel_id=1, source_target_pairs={{0,4},{4,8},{8,12},{12,16},{16,20},{20,24},{24,28},{28,0},{1,5},{5... | collective-permute-start | bytes 24584 | tf_op jit(solution)/shard_map/ppermute | solution.py:88
  95.4 6.4 %collective-permute-start.2 = (bf16[1,4096]{1,0:T(2,128)(2,1)S(1)}, bf16[1,4096]{1,0:T(2,128)(2,1)S(1)}, u32[]{:S(2)}, u32[]{:S(2)}) collective-permute-start(bf16[1,4096]{1,0:T(2,128)(2,1)S(1)} %collective-permute-done.1), channel_id=1, source_target_pairs={{0,4},{4,8},{8,12},{12,16},{16,20},{20,24},{24,28},{28,0},{1,5},{5... | collective-permute-start | bytes 24584 | tf_op jit(solution)/shard_map/ppermute | solution.py:88
  101.8 6.4 %collective-permute-start.3 = (bf16[1,4096]{1,0:T(2,128)(2,1)S(1)}, bf16[1,4096]{1,0:T(2,128)(2,1)S(1)}, u32[]{:S(2)}, u32[]{:S(2)}) collective-permute-start(bf16[1,4096]{1,0:T(2,128)(2,1)S(1)} %collective-permute-done.2), channel_id=1, source_target_pairs={{0,4},{4,8},{8,12},{12,16},{16,20},{20,24},{24,28},{28,0},{1,5},{5... | collective-permute-start | bytes 24584 | tf_op jit(solution)/shard_map/ppermute | solution.py:88
  108.3 6.4 %collective-permute-start.4 = (bf16[1,4096]{1,0:T(2,128)(2,1)S(1)}, bf16[1,4096]{1,0:T(2,128)(2,1)S(1)}, u32[]{:S(2)}, u32[]{:S(2)}) collective-permute-start(bf16[1,4096]{1,0:T(2,128)(2,1)S(1)} %collective-permute-done.3), channel_id=1, source_target_pairs={{0,4},{4,8},{8,12},{12,16},{16,20},{20,24},{24,28},{28,0},{1,5},{5... | collective-permute-start | bytes 24584 | tf_op jit(solution)/shard_map/ppermute | solution.py:88
  114.7 6.4 %collective-permute-start.5 = (bf16[1,4096]{1,0:T(2,128)(2,1)S(1)}, bf16[1,4096]{1,0:T(2,128)(2,1)S(1)}, u32[]{:S(2)}, u32[]{:S(2)}) collective-permute-start(bf16[1,4096]{1,0:T(2,128)(2,1)S(1)} %collective-permute-done.4), channel_id=1, source_target_pairs={{0,4},{4,8},{8,12},{12,16},{16,20},{20,24},{24,28},{28,0},{1,5},{5... | collective-permute-start | bytes 24584 | tf_op jit(solution)/shard_map/ppermute | solution.py:88
  121.1 6.4 %collective-permute-start.6 = (bf16[1,4096]{1,0:T(2,128)(2,1)S(1)}, bf16[1,4096]{1,0:T(2,128)(2,1)S(1)}, u32[]{:S(2)}, u32[]{:S(2)}) collective-permute-start(bf16[1,4096]{1,0:T(2,128)(2,1)S(1)} %collective-permute-done.5), channel_id=1, source_target_pairs={{0,4},{4,8},{8,12},{12,16},{16,20},{20,24},{24,28},{28,0},{1,5},{5... | collective-permute-start | bytes 24584 | tf_op jit(solution)/shard_map/ppermute | solution.py:88
